TPU v7x, 256 devices: a whole 4x4x8 slice. The times are simulated.
256 devices in a mesh: tm: 32 (over x, z), chan: 8 (over y, core).
Axes of the slice: x: 4, y: 4, z: 8, core: 2. Of those that a mesh axis runs over, the one named last changes fastest.
Arguments:
- visibilities: bfloat16 [32, 8, 512, 1024], P('tm', None, None, 'chan'), may hold values from -6 to 6
- station_gains: float32 [8, 192, 1024], P(None, 'chan'), may hold values from -1.5 to 1.5, as said below
- station_pairs: int32 [512, 2], replicated, may hold values from 0 to 191, as said below
- average_bands: int32 [512, 2], replicated, may hold values from 0 to 3, as said below
- tile_map: int32 [512, 32], replicated, may hold values from 0 to 255
- baseline_order: int32 [512], replicated, may hold values from 0 to 511, as said below
Outputs:
- averaged: bfloat16 [32, 8, 512, 1024], P(None, None, 'tm', 'chan')
- gridded: float32 [256, 8, 1024], P('tm', None, 'chan')
Inputs may be any that keep to these rules, and one draw needn't show every extreme that they name: `station_pairs`: row b holds the two stations of baseline b, the first smaller than the second. `average_bands`: column 0 is at most 3, column 1 at most 2. In each aligned block of 16 positions k of baseline_order, the bands of the baselines baseline_order[k] are, in some order, the pairs (3 - j % (3 + 1), 2 - j % (2 + 1)) for j = 0 to 15. `baseline_order`: each baseline once. `station_gains`: diagonal Jones entries have magnitudes of order one.
All inputs are finite; a program needn't handle non-finite values.
Results may differ from a plain program's by a relative error of at most 0.019.
Values may be sent and summed in bfloat16 or wider, within the bound.
No kernel may reach another device: no remote copies, remote signals or barrier semaphores. Data moves between devices by JAX's collectives and lax.ppermute only.
A program may use at most 128 MiB of HBM per device.

v0:
```python
import jax
import jax.numpy as jnp
from jax import lax
from jax.sharding import PartitionSpec as P

TILE_DEV = 8
TLOG = 3
CLOG = 2


def product(left, right):
    return (left[0] * right[0] - left[1] * right[1], left[0] * right[1] + left[1] * right[0])


def product_conj(left, right):
    return (left[0] * right[0] + left[1] * right[1], left[1] * right[0] - left[0] * right[1])


def add_pair(left, right):
    return (left[0] + right[0], left[1] + right[1])


def as_matrix(components):
    return [
        [(components[0], components[1]), (components[2], components[3])],
        [(components[4], components[5]), (components[6], components[7])],
    ]


def jones_apply(first, middle, second):
    left_gain = as_matrix(first)
    coherency = as_matrix(middle)
    right_gain = as_matrix(second)
    partial_rows = [
        [
            add_pair(
                product(left_gain[i][0], coherency[0][k]), product(left_gain[i][1], coherency[1][k])
            )
            for k in range(2)
        ]
        for i in range(2)
    ]
    result = []
    for i in range(2):
        for c in range(2):
            element = add_pair(
                product_conj(partial_rows[i][0], right_gain[c][0]),
                product_conj(partial_rows[i][1], right_gain[c][1]),
            )
            result.extend(element)
    return result


def calibrate(samples, gain_table, first_station, second_station):
    left_gain = jnp.take(gain_table, first_station, axis=1)
    right_gain = jnp.take(gain_table, second_station, axis=1)
    values = [samples[:, i].astype(jnp.float32) for i in range(8)]
    result = jones_apply(
        [left_gain[i][None] for i in range(8)], values, [right_gain[i][None] for i in range(8)]
    )
    return jnp.stack(result, axis=1).astype(jnp.bfloat16)


def halve_time(current, size):
    extent = current.shape[0]
    shaped = current.reshape((extent // size, 2, size // 2) + current.shape[1:])
    merged = 0.5 * (shaped[:, 0:1] + shaped[:, 1:2])
    return jnp.broadcast_to(merged, shaped.shape).reshape(current.shape)


def halve_chan(current, size):
    extent = current.shape[-1]
    shaped = current.reshape(current.shape[:-1] + (extent // size, 2, size // 2))
    merged = 0.5 * (shaped[..., 0:1, :] + shaped[..., 1:2, :])
    return jnp.broadcast_to(merged, shaped.shape).reshape(current.shape)


def band_average(samples, time_levels, chan_levels):
    values = samples.astype(jnp.float32)
    time_select = time_levels[None, None, :, None]
    chan_select = chan_levels[None, None, :, None]
    result = values
    current = values
    for k in range(1, TLOG + 1):
        current = halve_time(current, 2**k)
        result = jnp.where(time_select >= k, current, result)
    final = result
    current = result
    for k in range(1, CLOG + 1):
        current = halve_chan(current, 2**k)
        final = jnp.where(chan_select >= k, current, final)
    return final.astype(jnp.bfloat16)


def shards(visibilities, station_gains, station_pairs, average_bands, tile_map, baseline_order):
    chan_width = visibilities.shape[3]
    block_size = visibilities.shape[2] // lax.axis_size("tm")
    all_gains = lax.all_gather(station_gains, "chan", axis=1, tiled=True)
    gain_table = lax.dynamic_slice_in_dim(
        all_gains, lax.axis_index("chan") * chan_width, chan_width, 2
    )
    reordered = jnp.take(visibilities, baseline_order, axis=2)
    rows_here = lax.dynamic_slice_in_dim(
        baseline_order, lax.axis_index("tm") * block_size, block_size
    )
    bands_here = average_bands[rows_here]
    ordered_pairs = station_pairs[baseline_order]
    payload = calibrate(reordered, gain_table, ordered_pairs[:, 0], ordered_pairs[:, 1])
    turned = lax.all_to_all(payload, "tm", split_axis=2, concat_axis=0, tiled=True)
    averaged = band_average(turned, bands_here[:, 0], bands_here[:, 1])
    tile_here = tile_map[rows_here].T
    time_index = jnp.arange(averaged.shape[0], dtype=jnp.int32)[:, None]
    period = jnp.left_shift(jnp.ones_like(bands_here[:, 0]), bands_here[:, 0])[None, :]
    tile_ids = jnp.where(time_index % period == 0, tile_here, -1)
    targets = jnp.arange(TILE_DEV * lax.axis_size("tm"), dtype=jnp.int32)
    one_hot = (tile_ids[None] == targets[:, None, None]).astype(jnp.bfloat16)
    gridded = lax.psum_scatter(
        jnp.einsum("rtb,tkbc->rkc", one_hot, averaged, preferred_element_type=jnp.float32).astype(
            jnp.bfloat16
        ),
        "tm",
        scatter_dimension=0,
        tiled=True,
    ).astype(jnp.float32)
    return (averaged, gridded)


def solution(mesh):
    return jax.shard_map(
        shards,
        mesh=mesh,
        in_specs=(P("tm", None, None, "chan"), P(None, "chan", None), P(), P(), P(), P()),
        out_specs=(P(None, None, "tm", "chan"), P("tm", None, "chan")),
        check_vma=False,
    )
```

profile of v0, /device:TPU:8, one launch (start us, length us, event | category | flops | bytes accessed | tf_op | source)
XLA Modules:
  0.0 475.1 jit_solution(13990417689148985308)
XLA Ops:
  7.2 2.5 copy.586
  11.8 1.8 gather_fusion.2
  14.1 41.8 %all-gather.2.cloned.1.call-done = f32[8,192,1024]{2,0,1:T(8,128)} async-done(((f32[8,24,1024]{2,0,1:T(8,128)}), f32[8,192,1024]{2,0,1:T(8,128)}) %all-gather.2.cloned.1.call-update) | async-done | bytes 6291472 | tf_op jit(solution)/shard_map/all_gather | solution.py:98
  57.1 2.7 gather_fusion.5
  59.8 2.7 gather_fusion.4
  62.5 2.2 fusion.11
  68.5 9.8 %all-to-all-start = ((bf16[1,8,512,128]{3,1,0,2:T(8,128)(2,1)}), bf16[1,8,512,128]{3,1,0,2:T(8,128)(2,1)S(1)}, u32[]{:S(2)}, u32[]{:S(2)}) async-start(bf16[1,8,512,128]{3,1,0,2:T(8,128)(2,1)} %copy.591), calls=%async_computation | async-start | bytes 2097152 | tf_op jit(solution)/shard_map/all_to_all | solution.py:109
  81.0 26.3 %all-to-all-done = bf16[1,8,512,128]{3,1,0,2:T(8,128)(2,1)S(1)} async-done(((bf16[1,8,512,128]{3,1,0,2:T(8,128)(2,1)}), bf16[1,8,512,128]{3,1,0,2:T(8,128)(2,1)S(1)}, u32[]{:S(2)}, u32[]{:S(2)}) %all-to-all-start) | async-done | bytes 1048608 | tf_op jit(solution)/shard_map/all_to_all | solution.py:109
  110.6 2.8 copy.621
  113.3 2.6 copy.620
  116.0 5.8 %add_multiply_fusion = f32[8,1,8,16,128]{3,2,4,0,1:T(8,128)} fusion(f32[8,1,8,16,128]{3,2,4,0,1:T(8,128)} %copy.620, f32[8,1,8,16,128]{3,2,4,0,1:T(8,128)} %copy.621), kind=kLoop, calls=%fused_computation.7 | loop fusion | flops 262144 | bytes 1572864 | tf_op jit(solution)/shard_map/mul | solution.py:67
  121.8 2.7 copy.625
  124.5 2.4 fusion.5
  127.6 6.6 %copy.598 = f32[32,1,8,16,128]{0,3,4,2,1:T(8,128)} copy(f32[32,1,8,16,128]{4,3,0,2,1:T(8,128)} %convert_bitcast_fusion) | data formatting | bytes 4194304 | tf_op jit(solution)/shard_map/convert_element_type | solution.py:79
  134.2 8.7 %copy.600 = f32[32,8,16,64,2,1]{3,2,5,4,1,0:T(8,128)} copy(f32[32,8,16,64,2,1]{0,2,4,3,1,5:T(8,128)} %bitcast.225) | data formatting | bytes 4194304 | tf_op jit(solution)/shard_map/convert_element_type | solution.py:79
  142.9 6.0 %copy.597 = f32[16,8,16,128]{2,1,3,0:T(8,128)} copy(f32[16,8,16,128]{3,2,0,1:T(8,128)} %fusion.59) | data formatting | bytes 2097152 | tf_op jit(solution)/shard_map/broadcast_in_dim | solution.py:68
  148.9 11.0 %broadcast_in_dim.122 = f32[16,2,8,16,128]{3,2,4,1,0:T(8,128)} broadcast(f32[16,8,16,128]{2,1,3,0:T(8,128)} %copy.597), dimensions={0,2,3,4} | broadcast | bytes 3145728 | tf_op jit(solution)/shard_map/broadcast_in_dim | solution.py:68
  159.9 11.9 %copy.599 = f32[32,8,16,64,2,1]{3,2,5,4,1,0:T(8,128)} copy(f32[32,8,16,64,2,1]{2,1,4,3,0,5:T(8,128)} %bitcast.219) | data formatting | bytes 4194304 | tf_op jit(solution)/shard_map/broadcast_in_dim | solution.py:68
  171.8 7.6 %broadcast_in_dim.117 = f32[4,2,4,8,16,128]{4,3,5,2,1,0:T(8,128)} broadcast(f32[4,8,16,128]{2,1,3,0:T(8,128)S(1)} %fusion.5), dimensions={0,3,4,5} | broadcast | bytes 2359296 | tf_op jit(solution)/shard_map/broadcast_in_dim | solution.py:68
  179.4 12.0 %copy.602 = f32[32,8,16,64,2,1]{3,2,5,4,1,0:T(8,128)} copy(f32[32,8,16,64,2,1]{2,1,4,3,0,5:T(8,128)} %bitcast.220) | data formatting | bytes 4194304 | tf_op jit(solution)/shard_map/reshape | solution.py:68
  191.4 10.2 %broadcast_in_dim.119 = f32[8,2,2,8,16,128]{4,3,5,2,1,0:T(8,128)} broadcast(f32[8,8,16,128]{2,1,3,0:T(8,128)} %bitcast.224), dimensions={0,3,4,5} | broadcast | bytes 2621440 | tf_op jit(solution)/shard_map/broadcast_in_dim | solution.py:68
  201.6 11.9 %copy.601 = f32[32,8,16,64,2,1]{3,2,5,4,1,0:T(8,128)} copy(f32[32,8,16,64,2,1]{2,1,4,3,0,5:T(8,128)} %bitcast.221) | data formatting | bytes 4194304 | tf_op jit(solution)/shard_map/reshape | solution.py:68
  213.5 8.0 %select_select_fusion = f32[32,8,16,64,2,1]{3,2,5,4,1,0:T(8,128)S(1)} fusion(f32[32,8,16,64,2,1]{3,2,5,4,1,0:T(8,128)} %copy.602, f32[32,8,16,64,2,1]{3,2,5,4,1,0:T(8,128)} %copy.601, f32[32,8,16,64,2,1]{3,2,5,4,1,0:T(8,128)} %copy.599, f32[32,8,16,64,2,1]{3,2,5,4,1,0:T(8,128)} %copy.600, pred[16]{0:T(512)(128)(4,1)S(1)} %get-tuple-element.31, ...), kind=kLoop, calls=%fused_computation.6 | loop fusion | flops 1572864 | bytes 10485808 | tf_op jit(solution)/shard_map/jit(_where)/select_n | solution.py:86
  221.6 1.7 fusion.58
  223.6 4.5 copy.606
  228.2 4.1 broadcast_in_dim.128
  232.3 6.1 %copy.610 = bf16[32,8,16,128]{3,2,0,1:T(8,128)(2,1)} copy(bf16[32,8,16,128]{0,2,3,1:T(8,128)(2,1)} %bitcast.228) | data formatting | bytes 2097152 | tf_op jit(solution)/shard_map/broadcast_in_dim | solution.py:75
  238.4 3.6 copy.603
  242.0 2.5 fusion.1
  244.5 2.5 broadcast_in_dim.125
  247.0 6.2 %copy.611 = bf16[32,8,16,128]{3,2,0,1:T(8,128)(2,1)} copy(bf16[32,8,16,128]{0,2,3,1:T(8,128)(2,1)} %bitcast.230) | data formatting | bytes 2097152 | tf_op jit(solution)/shard_map/reshape | solution.py:75
  258.5 208.4 %reduce-scatter.4.cloned.1.call-done = bf16[8,1024]{1,0:T(8,128)(2,1)} async-done(((bf16[256,1024]{1,0:T(8,128)(2,1)}), bf16[8,1024]{1,0:T(8,128)(2,1)}) %reduce-scatter.4.cloned.1.call-update) | async-done | bytes 16400
  (81 shorter events, 20.8 us)
Async XLA Ops:
  7.2 2.7 copy-start.9
  7.2 2.8 copy-start.4
  7.2 3.5 copy-start.6
  7.2 48.7 %all-gather.2.cloned.1.call-start = ((), (), s32[]{:S(2)}) async-start(), calls=%async_computation.2 | async-start | bytes 7077888 | tf_op jit(solution)/shard_map/all_gather | solution.py:98
  62.5 2.2 copy-start.1
  66.8 11.6 %copy-start.10 = (s32[512,2]{0,1:T(2,128)S(1)}, s32[512,2]{0,1:T(2,128)}, u32[]{:S(2)}) copy-start(s32[512,2]{0,1:T(2,128)} %param.11) | copy-start | bytes 12292
  66.8 11.7 %copy-start.5 = (s32[512,32]{0,1:T(8,128)S(1)}, s32[512,32]{0,1:T(8,128)}, u32[]{:S(2)}) copy-start(s32[512,32]{0,1:T(8,128)} %param.12) | copy-start | bytes 196612
  68.5 38.8 %all-to-all-start = ((bf16[1,8,512,128]{3,1,0,2:T(8,128)(2,1)}), bf16[1,8,512,128]{3,1,0,2:T(8,128)(2,1)S(1)}, u32[]{:S(2)}, u32[]{:S(2)}) async-start(bf16[1,8,512,128]{3,1,0,2:T(8,128)(2,1)} %copy.591), calls=%async_computation | async-start | bytes 2097152 | tf_op jit(solution)/shard_map/all_to_all | solution.py:109
  78.3 388.6 %reduce-scatter.4.cloned.1.call-start = ((), (), s32[]{:S(2)}) async-start(), calls=%async_computation.3 | async-start | bytes 540672
  201.6 11.9 %copy-start.7 = (pred[16]{0:T(512)(128)(4,1)S(1)}, pred[16]{0:T(512)(128)(4,1)}, u32[]{:S(2)}) copy-start(pred[16]{0:T(512)(128)(4,1)} %get-tuple-element.33) | copy-start | bytes 52
  247.0 6.2 %copy-start = (f32[16,8,16,128]{3,2,0,1:T(8,128)S(1)}, f32[16,8,16,128]{3,2,0,1:T(8,128)}, u32[]{:S(2)}) copy-start(f32[16,8,16,128]{3,2,0,1:T(8,128)} %fusion.59) | copy-start | bytes 3145732
  253.2 1.2 copy-start.2
  253.2 1.5 copy-start.3
  253.2 1.5 copy-start.8
  253.2 1.5 copy-start.11
  253.2 1.5 copy-start.12
Sparse Core Ops, SparseCore 0:
  10.4 45.4 all-gather.1
  257.4 209.4 reduce-scatter.3
where the time goes:
time: 476 us; the launch traced here: 475 us
  waiting for transfers between devices  276 us (58%)
  local copies, waits for them, and re-layouts  142 us (30%)
  other arithmetic  31.2 us (7%)
  between operations  14.4 us (3%)
  starting transfers between devices  9.9 us (2%)
    unnamed x3, waiting for transfers between devices  208 us
    broadcast_in_dim x8, local copies, waits for them, and re-layouts, halve_time(): return jnp.broadcast_to(merged, shaped.shape).reshape(current.shape)  47.1 us
    all_gather x1, waiting for transfers between devices, shards(): all_gains = lax.all_gather(station_gains, 'chan', axis=1, tiled=True)  41.8 us
    all_to_all x1, waiting for transfers between devices, shards(): lax.all_to_all(payload, 'tm', split_axis=2, concat_axis=0, tiled=True)  26.3 us
    reshape x2, local copies, waits for them, and re-layouts, halve_time(): return jnp.broadcast_to(merged, shaped.shape).reshape(current.shape)  23.9 us
    broadcast_in_dim x4, local copies, waits for them, and re-layouts, halve_chan(): return jnp.broadcast_to(merged, shaped.shape).reshape(current.shape)  17.2 us
    unnamed x38, local copies, waits for them, and re-layouts  16.4 us
    convert_element_type x2, local copies, waits for them, and re-layouts, band_average(): values = samples.astype(jnp.float32)  15.3 us
  transfers between devices with their start and end apart: 3, of which 3 were waited for; matrix products, arithmetic and copies ran while one was open for 2% of the time, Pallas kernels for 0%

commit v1 on v0

--- a/solution.py
+++ b/solution.py
@@ -95,7 +95,10 @@
 def shards(visibilities, station_gains, station_pairs, average_bands, tile_map, baseline_order):
     chan_width = visibilities.shape[3]
     block_size = visibilities.shape[2] // lax.axis_size("tm")
-    all_gains = lax.all_gather(station_gains, "chan", axis=1, tiled=True)
+    count = lax.axis_size("chan")
+    parts = jnp.stack([station_gains for _ in range(count)])
+    parts = lax.all_to_all(parts, "chan", split_axis=0, concat_axis=0)
+    all_gains = jnp.concatenate(parts, axis=1)
     gain_table = lax.dynamic_slice_in_dim(
         all_gains, lax.axis_index("chan") * chan_width, chan_width, 2
     )

time: 476 us -> 511 us (1.074)
  waiting for transfers between devices: 276 us -> 300 us
  starting transfers between devices: 9.9 us -> 16.6 us
    all_to_all x0 -> x1, waiting for transfers between devices: none -> 66.5 us  [shards(): parts = lax.all_to_all(parts, 'chan', split_axis=0, concat_axis=0)]
    all_gather x1 -> x0, waiting for transfers between devices: 41.8 us -> none  [shards(): all_gains = lax.all_gather(station_gains, 'chan', axis=1, tiled=True)]
    all_to_all x0 -> x1, starting transfers between devices: none -> 6.95 us  [shards(): parts = lax.all_to_all(parts, 'chan', split_axis=0, concat_axis=0)]
    unnamed x3 -> x2, waiting for transfers between devices: 208 us -> 208 us
where the time goes in v1:
time: 511 us; the launch traced here: 510 us
  waiting for transfers between devices  300 us (59%)
  local copies, waits for them, and re-layouts  147 us (29%)
  other arithmetic  31.2 us (6%)
  starting transfers between devices  16.6 us (3%)
  between operations  14.4 us (3%)
    unnamed x2, waiting for transfers between devices  208 us
    all_to_all x1, waiting for transfers between devices, shards(): parts = lax.all_to_all(parts, 'chan', split_axis=0, concat_axis=0)  66.5 us
    broadcast_in_dim x8, local copies, waits for them, and re-layouts, halve_time(): return jnp.broadcast_to(merged, shaped.shape).reshape(current.shape)  47.1 us
    all_to_all x1, waiting for transfers between devices, shards(): lax.all_to_all(payload, 'tm', split_axis=2, concat_axis=0, tiled=True)  25.8 us
    reshape x2, local copies, waits for them, and re-layouts, halve_time(): return jnp.broadcast_to(merged, shaped.shape).reshape(current.shape)  23.9 us
    broadcast_in_dim x4, local copies, waits for them, and re-layouts, halve_chan(): return jnp.broadcast_to(merged, shaped.shape).reshape(current.shape)  17.2 us
    convert_element_type x2, local copies, waits for them, and re-layouts, band_average(): values = samples.astype(jnp.float32)  15.4 us
    unnamed x38, local copies, waits for them, and re-layouts  14.3 us
  transfers between devices with their start and end apart: 3, of which 3 were waited for; matrix products, arithmetic and copies ran while one was open for 2% of the time, Pallas kernels for 0%

profile of v1, /device:TPU:8, one launch (start us, length us, event | category | flops | bytes accessed | tf_op | source)
XLA Modules:
  0.0 510.2 jit_solution(7312626645357967211)
XLA Ops:
  7.2 4.6 stack.38
  11.8 6.9 %all-to-all-start = ((f32[8,8,24,1024]{3,2,1,0:T(8,128)}), f32[8,8,24,1024]{3,2,1,0:T(8,128)}, u32[]{:S(2)}, u32[]{:S(2)}) async-start(f32[8,8,24,1024]{3,2,1,0:T(8,128)} %stack.38), calls=%async_computation | async-start | bytes 12582912 | tf_op jit(solution)/shard_map/all_to_all | solution.py:100
  23.0 66.5 %all-to-all-done = f32[8,8,24,1024]{3,2,1,0:T(8,128)} async-done(((f32[8,8,24,1024]{3,2,1,0:T(8,128)}), f32[8,8,24,1024]{3,2,1,0:T(8,128)}, u32[]{:S(2)}, u32[]{:S(2)}) %all-to-all-start) | async-done | bytes 6291488 | tf_op jit(solution)/shard_map/all_to_all | solution.py:100
  89.5 3.4 copy.587
  93.5 2.7 gather_fusion.5
  96.2 2.7 gather_fusion.4
  98.9 2.2 fusion.11
  104.9 9.6 %all-to-all-start.1 = ((bf16[1,8,512,128]{3,1,0,2:T(8,128)(2,1)}), bf16[1,8,512,128]{3,1,0,2:T(8,128)(2,1)S(1)}, u32[]{:S(2)}, u32[]{:S(2)}) async-start(bf16[1,8,512,128]{3,1,0,2:T(8,128)(2,1)} %copy.593), calls=%async_computation.1 | async-start | bytes 2097152 | tf_op jit(solution)/shard_map/all_to_all | solution.py:112
  117.2 25.8 %all-to-all-done.1 = bf16[1,8,512,128]{3,1,0,2:T(8,128)(2,1)S(1)} async-done(((bf16[1,8,512,128]{3,1,0,2:T(8,128)(2,1)}), bf16[1,8,512,128]{3,1,0,2:T(8,128)(2,1)S(1)}, u32[]{:S(2)}, u32[]{:S(2)}) %all-to-all-start.1) | async-done | bytes 1048608 | tf_op jit(solution)/shard_map/all_to_all | solution.py:112
  146.3 2.8 copy.624
  149.1 2.6 copy.623
  151.7 5.8 %add_multiply_fusion = f32[8,1,8,16,128]{3,2,4,0,1:T(8,128)} fusion(f32[8,1,8,16,128]{3,2,4,0,1:T(8,128)} %copy.623, f32[8,1,8,16,128]{3,2,4,0,1:T(8,128)} %copy.624), kind=kLoop, calls=%fused_computation.7 | loop fusion | flops 262144 | bytes 1572864 | tf_op jit(solution)/shard_map/mul | solution.py:67
  157.5 2.7 copy.628
  160.2 2.4 fusion.5
  163.3 6.6 %copy.600 = f32[32,1,8,16,128]{0,3,4,2,1:T(8,128)} copy(f32[32,1,8,16,128]{4,3,0,2,1:T(8,128)} %convert_bitcast_fusion) | data formatting | bytes 4194304 | tf_op jit(solution)/shard_map/convert_element_type | solution.py:79
  169.9 8.8 %copy.602 = f32[32,8,16,64,2,1]{3,2,5,4,1,0:T(8,128)} copy(f32[32,8,16,64,2,1]{0,2,4,3,1,5:T(8,128)} %bitcast.228) | data formatting | bytes 4194304 | tf_op jit(solution)/shard_map/convert_element_type | solution.py:79
  178.7 6.0 %copy.599 = f32[16,8,16,128]{2,1,3,0:T(8,128)} copy(f32[16,8,16,128]{3,2,0,1:T(8,128)} %fusion.59) | data formatting | bytes 2097152 | tf_op jit(solution)/shard_map/broadcast_in_dim | solution.py:68
  184.6 11.0 %broadcast_in_dim.122 = f32[16,2,8,16,128]{3,2,4,1,0:T(8,128)} broadcast(f32[16,8,16,128]{2,1,3,0:T(8,128)} %copy.599), dimensions={0,2,3,4} | broadcast | bytes 3145728 | tf_op jit(solution)/shard_map/broadcast_in_dim | solution.py:68
  195.6 12.0 %copy.601 = f32[32,8,16,64,2,1]{3,2,5,4,1,0:T(8,128)} copy(f32[32,8,16,64,2,1]{2,1,4,3,0,5:T(8,128)} %bitcast.222) | data formatting | bytes 4194304 | tf_op jit(solution)/shard_map/broadcast_in_dim | solution.py:68
  207.6 7.6 %broadcast_in_dim.117 = f32[4,2,4,8,16,128]{4,3,5,2,1,0:T(8,128)} broadcast(f32[4,8,16,128]{2,1,3,0:T(8,128)S(1)} %fusion.5), dimensions={0,3,4,5} | broadcast | bytes 2359296 | tf_op jit(solution)/shard_map/broadcast_in_dim | solution.py:68
  215.2 12.0 %copy.604 = f32[32,8,16,64,2,1]{3,2,5,4,1,0:T(8,128)} copy(f32[32,8,16,64,2,1]{2,1,4,3,0,5:T(8,128)} %bitcast.223) | data formatting | bytes 4194304 | tf_op jit(solution)/shard_map/reshape | solution.py:68
  227.1 10.2 %broadcast_in_dim.119 = f32[8,2,2,8,16,128]{4,3,5,2,1,0:T(8,128)} broadcast(f32[8,8,16,128]{2,1,3,0:T(8,128)} %bitcast.227), dimensions={0,3,4,5} | broadcast | bytes 2621440 | tf_op jit(solution)/shard_map/broadcast_in_dim | solution.py:68
  237.3 11.9 %copy.603 = f32[32,8,16,64,2,1]{3,2,5,4,1,0:T(8,128)} copy(f32[32,8,16,64,2,1]{2,1,4,3,0,5:T(8,128)} %bitcast.224) | data formatting | bytes 4194304 | tf_op jit(solution)/shard_map/reshape | solution.py:68
  249.2 8.0 %select_select_fusion = f32[32,8,16,64,2,1]{3,2,5,4,1,0:T(8,128)S(1)} fusion(f32[32,8,16,64,2,1]{3,2,5,4,1,0:T(8,128)} %copy.604, f32[32,8,16,64,2,1]{3,2,5,4,1,0:T(8,128)} %copy.603, f32[32,8,16,64,2,1]{3,2,5,4,1,0:T(8,128)} %copy.601, f32[32,8,16,64,2,1]{3,2,5,4,1,0:T(8,128)} %copy.602, pred[16]{0:T(512)(128)(4,1)S(1)} %get-tuple-element.31, ...), kind=kLoop, calls=%fused_computation.6 | loop fusion | flops 1572864 | bytes 10485808 | tf_op jit(solution)/shard_map/jit(_where)/select_n | solution.py:86
  259.4 4.5 copy.608
  263.9 4.1 broadcast_in_dim.128
  268.0 6.1 %copy.612 = bf16[32,8,16,128]{3,2,0,1:T(8,128)(2,1)} copy(bf16[32,8,16,128]{0,2,3,1:T(8,128)(2,1)} %bitcast.231) | data formatting | bytes 2097152 | tf_op jit(solution)/shard_map/broadcast_in_dim | solution.py:75
  274.1 3.6 copy.605
  277.7 2.5 fusion.1
  280.3 2.5 broadcast_in_dim.125
  282.8 6.2 %copy.613 = bf16[32,8,16,128]{3,2,0,1:T(8,128)(2,1)} copy(bf16[32,8,16,128]{0,2,3,1:T(8,128)(2,1)} %bitcast.233) | data formatting | bytes 2097152 | tf_op jit(solution)/shard_map/reshape | solution.py:75
  294.3 207.7 %reduce-scatter.4.cloned.1.call-done = bf16[8,1024]{1,0:T(8,128)(2,1)} async-done(((bf16[256,1024]{1,0:T(8,128)(2,1)}), bf16[8,1024]{1,0:T(8,128)(2,1)}) %reduce-scatter.4.cloned.1.call-update) | async-done | bytes 16400
  (82 shorter events, 23.7 us)
Async XLA Ops:
  11.8 7.0 %copy-start.9 = (s32[512,2]{0,1:T(2,128)S(1)}, s32[512,2]{0,1:T(2,128)}, u32[]{:S(2)}) copy-start(s32[512,2]{0,1:T(2,128)} %param.10) | copy-start | bytes 12292
  11.8 7.1 %copy-start.4 = (bf16[1,8,512,128]{3,2,1,0:T(8,128)(2,1)S(1)}, bf16[1,8,512,128]{3,2,1,0:T(8,128)(2,1)}, u32[]{:S(2)}) copy-start(bf16[1,8,512,128]{3,2,1,0:T(8,128)(2,1)} %param.8) | copy-start | bytes 3145732
  11.8 77.8 %all-to-all-start = ((f32[8,8,24,1024]{3,2,1,0:T(8,128)}), f32[8,8,24,1024]{3,2,1,0:T(8,128)}, u32[]{:S(2)}, u32[]{:S(2)}) async-start(f32[8,8,24,1024]{3,2,1,0:T(8,128)} %stack.38), calls=%async_computation | async-start | bytes 12582912 | tf_op jit(solution)/shard_map/all_to_all | solution.py:100
  18.7 0.9 copy-start.6
  98.9 2.2 copy-start.1
  103.2 11.3 %copy-start.10 = (s32[512,2]{0,1:T(2,128)S(1)}, s32[512,2]{0,1:T(2,128)}, u32[]{:S(2)}) copy-start(s32[512,2]{0,1:T(2,128)} %param.11) | copy-start | bytes 12292
  103.2 11.5 %copy-start.5 = (s32[512,32]{0,1:T(8,128)S(1)}, s32[512,32]{0,1:T(8,128)}, u32[]{:S(2)}) copy-start(s32[512,32]{0,1:T(8,128)} %param.12) | copy-start | bytes 196612
  104.9 38.1 %all-to-all-start.1 = ((bf16[1,8,512,128]{3,1,0,2:T(8,128)(2,1)}), bf16[1,8,512,128]{3,1,0,2:T(8,128)(2,1)S(1)}, u32[]{:S(2)}, u32[]{:S(2)}) async-start(bf16[1,8,512,128]{3,1,0,2:T(8,128)(2,1)} %copy.593), calls=%async_computation.1 | async-start | bytes 2097152 | tf_op jit(solution)/shard_map/all_to_all | solution.py:112
  114.4 387.5 %reduce-scatter.4.cloned.1.call-start = ((), (), s32[]{:S(2)}) async-start(), calls=%async_computation.3 | async-start | bytes 540672
  237.3 11.9 %copy-start.7 = (pred[16]{0:T(512)(128)(4,1)S(1)}, pred[16]{0:T(512)(128)(4,1)}, u32[]{:S(2)}) copy-start(pred[16]{0:T(512)(128)(4,1)} %get-tuple-element.33) | copy-start | bytes 52
  282.8 6.2 %copy-start = (f32[16,8,16,128]{3,2,0,1:T(8,128)S(1)}, f32[16,8,16,128]{3,2,0,1:T(8,128)}, u32[]{:S(2)}) copy-start(f32[16,8,16,128]{3,2,0,1:T(8,128)} %fusion.59) | copy-start | bytes 3145732
  289.0 1.2 copy-start.2
  289.0 1.5 copy-start.3
  289.0 1.5 copy-start.8
  289.0 1.5 copy-start.11
  289.0 1.5 copy-start.12
Sparse Core Ops, SparseCore 0:
  293.2 208.7 reduce-scatter.3
